TPU v7x, 512 devices: a whole 4x4x16 slice. The times are simulated.
512 devices in a mesh: index: 64 (over z, y), query: 8 (over x, core).
Axes of the slice: x: 4, y: 4, z: 16, core: 2. Of those that a mesh axis runs over, the one named last changes fastest.
Arguments:
- queries: bfloat16 [256, 32, 128], P('query'), may hold values from -6 to 6
- passages: bfloat16 [32768, 128, 128], P(('index', 'query')), may hold values from -0.5 to 0.5
- lengths: int32 [32768], P(('index', 'query')), may hold values from 1 to 128
- candidates: int32 [256, 1024], P('query', 'index'), may hold values from 0 to 32767, as said below
Outputs:
- scores: float32 [256, 1024], P('query', 'index')
Inputs may be any that keep to these rules, and one draw needn't show every extreme that they name: Block b is stored on the device of flat position b // 64 along index+query. The 32 x 16 candidates held by one device name blocks of any one storing device at most 2 times, and exactly 2 times for some storing device.
All inputs are finite; a program needn't handle non-finite values.
Results may differ from a plain program's by a relative error of at most 0.0003.
Values may be sent and summed in bfloat16 or wider, within the bound.
No kernel may reach another device: no remote copies, remote signals or barrier semaphores. Data moves between devices by JAX's collectives and lax.ppermute only.
A program may use at most 64 MiB of HBM per device.

v0:
```python
import math
import jax
import jax.numpy as jnp
from jax import lax
from jax.sharding import PartitionSpec as P


def score_slots(slot_rows, slot_blocks, passages, lengths):
    slot_total = slot_blocks.shape[0]
    group = math.gcd(slot_total, 128)
    token_count = passages.shape[1]

    def score_group(packed):
        query_rows, block_ids = packed
        safe_ids = jnp.maximum(block_ids, 0)
        block_rows = passages[safe_ids]
        similar = jnp.einsum(
            "gtd,gpd->gtp", query_rows, block_rows, preferred_element_type=jnp.float32
        )
        token_pos = lax.broadcasted_iota(jnp.int32, (1, 1, token_count), 2)
        live = token_pos < lengths[safe_ids][:, None, None]
        best = jnp.max(jnp.where(live, similar, -jnp.inf), axis=2)
        return jnp.where(block_ids >= 0, jnp.mean(best, axis=1), jnp.float32(0.0))

    grouped_rows = slot_rows.reshape((slot_total // group, group) + slot_rows.shape[1:])
    grouped_ids = slot_blocks.reshape(slot_total // group, group)
    results = lax.map(score_group, (grouped_rows, grouped_ids))
    return results.reshape(slot_total)


def shards(queries, passages, lengths, candidates):
    n_index = lax.axis_size("index")
    n_query = lax.axis_size("query")
    devices = n_index * n_query
    q_local, cand_local = candidates.shape
    blk_local = passages.shape[0]
    request_count = q_local * cand_local
    capacity = max(2, 2 * request_count // devices)
    slot_total = devices * capacity
    flat_ids = candidates.reshape(request_count)
    owner = flat_ids // blk_local
    position = jnp.arange(request_count, dtype=jnp.int32)
    earlier = (owner[None, :] == owner[:, None]) & (position[None, :] < position[:, None])
    owner_rank = jnp.sum(earlier, axis=1)
    target = owner * capacity + owner_rank
    slot_request = jnp.full((slot_total,), -1, jnp.int32).at[target].set(position)
    slot_used = slot_request >= 0
    safe_request = jnp.maximum(slot_request, 0)
    slot_block = jnp.where(slot_used, flat_ids[safe_request] % blk_local, -1)
    slot_query = jnp.where(slot_used, safe_request // cand_local, 0)
    grid_shape = (n_index, n_query, capacity)
    sent_rows = queries[slot_query].reshape(grid_shape + queries.shape[1:])
    got_rows, got_blocks = (
        lax.all_to_all(
            lax.all_to_all(sent_rows, "index", split_axis=0, concat_axis=0, tiled=True),
            "query",
            split_axis=1,
            concat_axis=1,
            tiled=True,
        ),
        lax.all_to_all(
            lax.all_to_all(
                slot_block.reshape(grid_shape), "index", split_axis=0, concat_axis=0, tiled=True
            ),
            "query",
            split_axis=1,
            concat_axis=1,
            tiled=True,
        ),
    )
    got_rows = got_rows.reshape((slot_total,) + queries.shape[1:])
    results = score_slots(got_rows, got_blocks.reshape(slot_total), passages, lengths)
    returned = lax.all_to_all(
        lax.all_to_all(
            results.reshape(grid_shape), "index", split_axis=0, concat_axis=0, tiled=True
        ),
        "query",
        split_axis=1,
        concat_axis=1,
        tiled=True,
    )
    return returned.reshape(slot_total)[target].reshape(q_local, cand_local)


def solution(mesh):
    in_specs = (
        P("query", None, None),
        P(("index", "query"), None, None),
        P(("index", "query")),
        P("query", "index"),
    )
    out_specs = P("query", "index")
    return jax.shard_map(shards, mesh=mesh, in_specs=in_specs, out_specs=out_specs, check_vma=False)
```

profile of v0, /device:TPU:1, one launch (start us, length us, event | category | flops | bytes accessed | tf_op | source)
XLA Modules:
  0.0 660.3 jit_solution(18072776988277648268)
XLA Ops:
  0.0 0.8 copy.40
  1.0 0.2 convert_reduce_fusion
  1.3 2.4 scatter_custom_fusion
  3.8 6.9 %gather_fusion.2 = s32[1024]{0:T(1024)S(1)} fusion(s32[512]{0:T(512)S(1)} %reshape.186, s32[1024]{0:T(1024)S(1)} %get-tuple-element.51), kind=kCustom, calls=%fused_computation.2 | custom fusion | bytes 12288 | tf_op jit(solution)/shard_map/gather | solution.py:49
  10.6 0.2 reshape.187
  10.9 1.1 copy.42
  11.9 19.3 %all-to-all-start = ((s32[64,8,2]{1,2,0:T(2,128)}), s32[64,8,2]{1,2,0:T(2,128)S(1)}, u32[]{:S(2)}, u32[]{:S(2)}) async-start(s32[64,8,2]{1,2,0:T(2,128)} %copy.42), calls=%async_computation | async-start | bytes 131072 | tf_op jit(solution)/shard_map/all_to_all | solution.py:62
  31.2 9.9 %gather_fusion.3 = bf16[1024,32,128]{2,1,0:T(8,128)(2,1)} fusion(bf16[32,32,128]{2,1,0:T(8,128)(2,1)S(1)} %copy-done, s32[1024]{0:T(1024)S(1)} %get-tuple-element.50), kind=kCustom, calls=%fused_computation.3 | custom fusion | bytes 16781312 | tf_op jit(solution)/shard_map/gather | solution.py:52
  41.1 4.1 all-to-all-done
  45.2 10.7 %all-to-all-start.2 = ((bf16[64,8,2,32,128]{4,3,2,1,0:T(8,128)(2,1)}), bf16[64,8,2,32,128]{4,3,2,1,0:T(8,128)(2,1)}, u32[]{:S(2)}, u32[]{:S(2)}) async-start(bf16[64,8,2,32,128]{4,3,2,1,0:T(8,128)(2,1)} %bitcast.24), calls=%async_computation.2 | async-start | bytes 16777216 | tf_op jit(solution)/shard_map/all_to_all | solution.py:55
  56.0 0.7 reshape.245
  56.7 360.2 %all-to-all-done.2 = bf16[64,8,2,32,128]{4,3,2,1,0:T(8,128)(2,1)} async-done(((bf16[64,8,2,32,128]{4,3,2,1,0:T(8,128)(2,1)}), bf16[64,8,2,32,128]{4,3,2,1,0:T(8,128)(2,1)}, u32[]{:S(2)}, u32[]{:S(2)}) %all-to-all-start.2) | async-done | bytes 8388640 | tf_op jit(solution)/shard_map/all_to_all | solution.py:55
  416.9 14.0 %all-to-all-start.1 = ((s32[8,1,128]{2,1,0:T(1,128)}), s32[8,1,128]{2,1,0:T(1,128)S(1)}, u32[]{:S(2)}, u32[]{:S(2)}) async-start(s32[8,1,128]{2,1,0:T(1,128)} %reshape.245), calls=%async_computation.1 | async-start | bytes 8192 | tf_op jit(solution)/shard_map/all_to_all | solution.py:61
  430.9 9.5 %copy.45 = bf16[64,8,2,32,128]{4,3,2,0,1:T(8,128)(2,1)} copy(bf16[64,8,2,32,128]{4,3,2,1,0:T(8,128)(2,1)} %all-to-all-done.2) | data formatting | bytes 16777216 | tf_op jit(solution)/shard_map/all_to_all | solution.py:55
  440.4 5.1 all-to-all-start.3
  445.5 0.5 broadcast.214
  446.0 0.6 reduce
  446.7 0.2 copy.44
  446.9 0.2 reshape_reshape.9
  447.1 92.1 %all-to-all-done.3 = bf16[64,8,2,32,128]{4,3,2,0,1:T(8,128)(2,1)} async-done(((bf16[64,8,2,32,128]{4,3,2,0,1:T(8,128)(2,1)}), bf16[64,8,2,32,128]{4,3,2,0,1:T(8,128)(2,1)}, u32[]{:S(2)}, u32[]{:S(2)}) %all-to-all-start.3) | async-done | bytes 8388640 | tf_op jit(solution)/shard_map/all_to_all | solution.py:54
  539.2 9.6 %copy.46 = bf16[64,8,2,32,128]{4,3,2,1,0:T(8,128)(2,1)} copy(bf16[64,8,2,32,128]{4,3,2,0,1:T(8,128)(2,1)} %all-to-all-done.3) | data formatting | bytes 16777216 | tf_op jit(solution)/shard_map/all_to_all | solution.py:54
  548.8 75.9 %while.10 = (s32[]{:T(128)}, f32[8,128]{1,0:T(8,128)S(1)}, s32[8,128]{1,0:T(8,128)S(1)}, s32[64]{0:T(128)S(1)}, bf16[8,128,32,128]{3,2,1,0:T(8,128)(2,1)}, /*ind...) while((s32[]{:T(128)}, f32[8,128]{1,0:T(8,128)S(1)}, s32[8,128]{1,0:T(8,128)S(1)}, ...), condition=%wide.region_5.6_spmd, body=%wide.region_2.5_spmd.sunk | while | flops 135284096 | bytes 13708909 | solution.py:27
  548.9 3.1 gather_fusion
  551.9 1.2 gather_fusion.1
  553.2 4.9 select_reduce_fusion.2
  558.1 0.1 reduce_sum.24
  558.3 3.1 gather_fusion
  561.4 1.2 gather_fusion.1
  562.7 4.9 select_reduce_fusion.2
  567.6 0.1 reduce_sum.24
  567.8 3.1 gather_fusion
  570.9 1.2 gather_fusion.1
  572.2 4.9 select_reduce_fusion.2
  577.1 0.1 reduce_sum.24
  577.3 3.1 gather_fusion
  580.4 1.2 gather_fusion.1
  581.7 4.9 select_reduce_fusion.2
  586.6 0.1 reduce_sum.24
  586.8 3.1 gather_fusion
  589.9 1.2 gather_fusion.1
  591.2 4.9 select_reduce_fusion.2
  596.1 0.1 reduce_sum.24
  596.3 3.1 gather_fusion
  599.4 1.2 gather_fusion.1
  600.7 4.9 select_reduce_fusion.2
  605.6 0.1 reduce_sum.24
  605.8 3.1 gather_fusion
  608.9 1.2 gather_fusion.1
  610.2 4.9 select_reduce_fusion.2
  615.3 3.1 gather_fusion
  618.3 1.2 gather_fusion.1
  619.7 4.9 select_reduce_fusion.2
  624.7 0.2 reshape_reshape.11
  624.9 0.4 copy.47
  625.4 19.3 %all_to_all.30 = f32[64,8,2]{1,2,0:T(2,128)S(1)} all-to-all(f32[64,8,2]{1,2,0:T(2,128)S(1)} %copy.47), channel_id=1, replica_groups=mesh['index'=64,'query'=8] {'index'}, dimensions={0} | all-to-all | bytes 8192 | tf_op jit(solution)/shard_map/all_to_all | solution.py:74
  644.8 0.7 reshape.247
  645.5 5.7 all-to-all-start.5
  651.2 4.5 all-to-all-done.5
  655.7 0.5 broadcast.215
  656.2 0.7 reduce.1
  656.9 0.2 copy.49
  657.1 0.2 reshape.189
  657.3 2.3 gather_fusion.4
  659.7 0.7 copy.50
  (63 shorter events, 2.0 us)
Async XLA Ops:
  0.0 31.2 %copy-start = (bf16[32,32,128]{2,1,0:T(8,128)(2,1)S(1)}, bf16[32,32,128]{2,1,0:T(8,128)(2,1)}, u32[]{:S(2)}) copy-start(bf16[32,32,128]{2,1,0:T(8,128)(2,1)} %param.6) | copy-start | bytes 786436
  11.9 33.3 %all-to-all-start = ((s32[64,8,2]{1,2,0:T(2,128)}), s32[64,8,2]{1,2,0:T(2,128)S(1)}, u32[]{:S(2)}, u32[]{:S(2)}) async-start(s32[64,8,2]{1,2,0:T(2,128)} %copy.42), calls=%async_computation | async-start | bytes 131072 | tf_op jit(solution)/shard_map/all_to_all | solution.py:62
  45.2 371.7 %all-to-all-start.2 = ((bf16[64,8,2,32,128]{4,3,2,1,0:T(8,128)(2,1)}), bf16[64,8,2,32,128]{4,3,2,1,0:T(8,128)(2,1)}, u32[]{:S(2)}, u32[]{:S(2)}) async-start(bf16[64,8,2,32,128]{4,3,2,1,0:T(8,128)(2,1)} %bitcast.24), calls=%async_computation.2 | async-start | bytes 16777216 | tf_op jit(solution)/shard_map/all_to_all | solution.py:55
  416.9 23.5 %all-to-all-start.1 = ((s32[8,1,128]{2,1,0:T(1,128)}), s32[8,1,128]{2,1,0:T(1,128)S(1)}, u32[]{:S(2)}, u32[]{:S(2)}) async-start(s32[8,1,128]{2,1,0:T(1,128)} %reshape.245), calls=%async_computation.1 | async-start | bytes 8192 | tf_op jit(solution)/shard_map/all_to_all | solution.py:61
  440.4 98.8 %all-to-all-start.3 = ((bf16[64,8,2,32,128]{4,3,2,0,1:T(8,128)(2,1)}), bf16[64,8,2,32,128]{4,3,2,0,1:T(8,128)(2,1)}, u32[]{:S(2)}, u32[]{:S(2)}) async-start(bf16[64,8,2,32,128]{4,3,2,0,1:T(8,128)(2,1)} %copy.45), calls=%async_computation.3 | async-start | bytes 16777216 | tf_op jit(solution)/shard_map/all_to_all | solution.py:54
  447.1 101.8 %copy-start.1 = (s32[64]{0:T(128)S(1)}, s32[64]{0:T(128)}, u32[]{:S(2)}) copy-start(s32[64]{0:T(128)} %param.8) | copy-start | bytes 772
  447.1 101.8 %copy-start.2 = (bf16[64,128,128]{2,1,0:T(8,128)(2,1)S(1)}, bf16[64,128,128]{2,1,0:T(8,128)(2,1)}, u32[]{:S(2)}) copy-start(bf16[64,128,128]{2,1,0:T(8,128)(2,1)} %param.7) | copy-start | bytes 6291460
  645.5 10.2 %all-to-all-start.5 = ((f32[8,1,128]{2,1,0:T(1,128)}), f32[8,1,128]{2,1,0:T(1,128)S(1)}, u32[]{:S(2)}, u32[]{:S(2)}) async-start(f32[8,1,128]{2,1,0:T(1,128)} %reshape.247), calls=%async_computation.5 | async-start | bytes 8192 | tf_op jit(solution)/shard_map/all_to_all | solution.py:73
where the time goes:
time: 661 us; the launch traced here: 660 us
  waiting for transfers between devices  461 us (70%)
  local copies, waits for them, and re-layouts  82.2 us (12%)
  starting transfers between devices  54.7 us (8%)
  matrix products  39.1 us (6%)
  blocking collectives  19.3 us (3%)
    all_to_all x1, waiting for transfers between devices, shards(): lax.all_to_all(sent_rows, 'index', split_axis=0, concat_axis=0, tiled=True)  360 us
    all_to_all x1, waiting for transfers between devices, shards(): lax.all_to_all(lax.all_to_all(sent_rows, 'index', split_axis=0, concat_ax...  92.1 us
    dot_general x8, matrix products, score_group(): jnp.einsum('gtd,gpd->gtp', query_rows, block_rows, preferred_element_type...  39.1 us
    gather x8, local copies, waits for them, and re-layouts, score_group(): block_rows = passages[safe_ids]  24.5 us
    all_to_all x1, blocking collectives, shards(): lax.all_to_all(results.reshape(grid_shape), 'index', split_axis=0, concat...  19.3 us
    all_to_all x1, starting transfers between devices, shards(): lax.all_to_all(slot_block.reshape(grid_shape), 'index', split_axis=0, con...  19.3 us
    all_to_all x1, starting transfers between devices, shards(): lax.all_to_all(lax.all_to_all(slot_block.reshape(grid_shape), 'index', sp...  14 us
  transfers between devices with their start and end apart: 5, of which 4 were waited for; matrix products, arithmetic and copies ran while one was open for 3% of the time, Pallas kernels for 0%

commit v1 on v0

--- a/solution.py
+++ b/solution.py
@@ -3,6 +3,22 @@
 import jax.numpy as jnp
 from jax import lax
 from jax.sharding import PartitionSpec as P
+
+
+def exchange_in_pairs(array, axis, split, join):
+    ways, here = (lax.axis_size(axis), lax.axis_index(axis))
+    width = array.shape[split] // ways
+    dims = list(array.shape)
+    dims[split] = width
+    height = dims[join]
+    dims[join] = height * ways
+    full = jnp.zeros(dims, array.dtype)
+    for mask in range(ways):
+        part = lax.dynamic_slice_in_dim(array, (here ^ mask) * width, width, axis=split)
+        if mask:
+            part = lax.ppermute(part, axis, [(d, d ^ mask) for d in range(ways)])
+        full = lax.dynamic_update_slice_in_dim(full, part, (here ^ mask) * height, axis=join)
+    return full
 
 
 def score_slots(slot_rows, slot_blocks, passages, lengths):
@@ -70,14 +86,13 @@
     )
     got_rows = got_rows.reshape((slot_total,) + queries.shape[1:])
     results = score_slots(got_rows, got_blocks.reshape(slot_total), passages, lengths)
-    returned = lax.all_to_all(
+    returned = exchange_in_pairs(
         lax.all_to_all(
             results.reshape(grid_shape), "index", split_axis=0, concat_axis=0, tiled=True
         ),
         "query",
-        split_axis=1,
-        concat_axis=1,
-        tiled=True,
+        1,
+        1,
     )
     return returned.reshape(slot_total)[target].reshape(q_local, cand_local)
 

time: 661 us -> 679 us (1.027)
  starting transfers between devices: 54.7 us -> 78.1 us
  blocking collectives: 19.3 us -> 0 us
  waiting for transfers between devices: 461 us -> 471 us
    ppermute x0 -> x7, starting transfers between devices: none -> 23.5 us  [exchange_in_pairs(): part = lax.ppermute(part, axis, [(d, d ^ mask) for d in range(ways)])]
    all_to_all x1 -> x0, blocking collectives: 19.3 us -> none  [shards(): lax.all_to_all(results.reshape(grid_shape), 'index', split_axis=0, concat...]
    all_to_all x1, waiting for transfers between devices: 4.51 us -> 14 us  [shards(): lax.all_to_all(results.reshape(grid_shape), 'index', split_axis=0, concat...]
  transfers between devices with their start and end apart: 5 -> 12, of which waited for: 4 -> 4; matrix products, arithmetic and copies ran while one was open for 3% -> 4% of each run, Pallas kernels for 0% -> 0%
where the time goes in v1:
time: 679 us; the launch traced here: 678 us
  waiting for transfers between devices  471 us (69%)
  local copies, waits for them, and re-layouts  86.9 us (13%)
  starting transfers between devices  78.1 us (12%)
  matrix products  39.1 us (6%)
    all_to_all x1, waiting for transfers between devices, shards(): lax.all_to_all(sent_rows, 'index', split_axis=0, concat_axis=0, tiled=True)  360 us
    all_to_all x1, waiting for transfers between devices, shards(): lax.all_to_all(lax.all_to_all(sent_rows, 'index', split_axis=0, concat_ax...  92.1 us
    dot_general x8, matrix products, score_group(): jnp.einsum('gtd,gpd->gtp', query_rows, block_rows, preferred_element_type...  39.1 us
    gather x8, local copies, waits for them, and re-layouts, score_group(): block_rows = passages[safe_ids]  24.5 us
    ppermute x7, starting transfers between devices, exchange_in_pairs(): part = lax.ppermute(part, axis, [(d, d ^ mask) for d in range(ways)])  23.5 us
    all_to_all x1, starting transfers between devices, shards(): lax.all_to_all(slot_block.reshape(grid_shape), 'index', split_axis=0, con...  19.3 us
    all_to_all x1, waiting for transfers between devices, shards(): lax.all_to_all(results.reshape(grid_shape), 'index', split_axis=0, concat...  14 us
    all_to_all x1, starting transfers between devices, shards(): lax.all_to_all(lax.all_to_all(slot_block.reshape(grid_shape), 'index', sp...  14 us
  transfers between devices with their start and end apart: 12, of which 4 were waited for; matrix products, arithmetic and copies ran while one was open for 4% of the time, Pallas kernels for 0%

profile of v1, /device:TPU:1, one launch (start us, length us, event | category | flops | bytes accessed | tf_op | source)
XLA Modules:
  0.0 678.2 jit_solution(2234275111322504330)
XLA Ops:
  0.0 0.8 copy.58
  1.0 0.2 convert_reduce_fusion
  1.3 2.4 scatter_custom_fusion
  3.8 6.9 %gather_fusion.2 = s32[1024]{0:T(1024)S(1)} fusion(s32[512]{0:T(512)S(1)} %reshape.186, s32[1024]{0:T(1024)S(1)} %get-tuple-element.59), kind=kCustom, calls=%fused_computation.2 | custom fusion | bytes 12288 | tf_op jit(solution)/shard_map/gather | solution.py:65
  10.9 1.1 copy.60
  11.9 19.3 %all-to-all-start = ((s32[64,8,2]{1,2,0:T(2,128)}), s32[64,8,2]{1,2,0:T(2,128)S(1)}, u32[]{:S(2)}, u32[]{:S(2)}) async-start(s32[64,8,2]{1,2,0:T(2,128)} %copy.60), calls=%async_computation | async-start | bytes 131072 | tf_op jit(solution)/shard_map/all_to_all | solution.py:78
  31.2 9.8 %gather_fusion.3 = bf16[1024,32,128]{2,1,0:T(8,128)(2,1)} fusion(bf16[32,32,128]{2,1,0:T(8,128)(2,1)S(1)} %copy-done, s32[1024]{0:T(1024)S(1)} %get-tuple-element.58), kind=kCustom, calls=%fused_computation.3 | custom fusion | bytes 16781312 | tf_op jit(solution)/shard_map/gather | solution.py:68
  41.0 4.1 all-to-all-done
  45.2 10.7 %all-to-all-start.2 = ((bf16[64,8,2,32,128]{4,3,2,1,0:T(8,128)(2,1)}), bf16[64,8,2,32,128]{4,3,2,1,0:T(8,128)(2,1)}, u32[]{:S(2)}, u32[]{:S(2)}) async-start(bf16[64,8,2,32,128]{4,3,2,1,0:T(8,128)(2,1)} %bitcast.22), calls=%async_computation.2 | async-start | bytes 16777216 | tf_op jit(solution)/shard_map/all_to_all | solution.py:71
  55.9 0.7 reshape.245
  56.6 360.2 %all-to-all-done.2 = bf16[64,8,2,32,128]{4,3,2,1,0:T(8,128)(2,1)} async-done(((bf16[64,8,2,32,128]{4,3,2,1,0:T(8,128)(2,1)}), bf16[64,8,2,32,128]{4,3,2,1,0:T(8,128)(2,1)}, u32[]{:S(2)}, u32[]{:S(2)}) %all-to-all-start.2) | async-done | bytes 8388640 | tf_op jit(solution)/shard_map/all_to_all | solution.py:71
  416.9 14.0 %all-to-all-start.1 = ((s32[8,1,128]{2,1,0:T(1,128)}), s32[8,1,128]{2,1,0:T(1,128)S(1)}, u32[]{:S(2)}, u32[]{:S(2)}) async-start(s32[8,1,128]{2,1,0:T(1,128)} %reshape.245), calls=%async_computation.1 | async-start | bytes 8192 | tf_op jit(solution)/shard_map/all_to_all | solution.py:77
  430.9 9.5 %copy.63 = bf16[64,8,2,32,128]{4,3,2,0,1:T(8,128)(2,1)} copy(bf16[64,8,2,32,128]{4,3,2,1,0:T(8,128)(2,1)} %all-to-all-done.2) | data formatting | bytes 16777216 | tf_op jit(solution)/shard_map/all_to_all | solution.py:71
  440.4 5.1 all-to-all-start.3
  445.5 0.5 broadcast.222
  446.0 0.6 reduce
  447.1 92.1 %all-to-all-done.3 = bf16[64,8,2,32,128]{4,3,2,0,1:T(8,128)(2,1)} async-done(((bf16[64,8,2,32,128]{4,3,2,0,1:T(8,128)(2,1)}), bf16[64,8,2,32,128]{4,3,2,0,1:T(8,128)(2,1)}, u32[]{:S(2)}, u32[]{:S(2)}) %all-to-all-start.3) | async-done | bytes 8388640 | tf_op jit(solution)/shard_map/all_to_all | solution.py:70
  539.2 9.6 %copy.64 = bf16[64,8,2,32,128]{4,3,2,1,0:T(8,128)(2,1)} copy(bf16[64,8,2,32,128]{4,3,2,0,1:T(8,128)(2,1)} %all-to-all-done.3) | data formatting | bytes 16777216 | tf_op jit(solution)/shard_map/all_to_all | solution.py:70
  548.8 75.9 %while.10 = (s32[]{:T(128)}, f32[8,128]{1,0:T(8,128)S(1)}, s32[8,128]{1,0:T(8,128)S(1)}, s32[64]{0:T(128)S(1)}, bf16[8,128,32,128]{3,2,1,0:T(8,128)(2,1)}, /*ind...) while((s32[]{:T(128)}, f32[8,128]{1,0:T(8,128)S(1)}, s32[8,128]{1,0:T(8,128)S(1)}, ...), condition=%wide.region_5.6_spmd, body=%wide.region_2.5_spmd.sunk | while | flops 135284096 | bytes 13708909 | solution.py:43
  548.9 3.1 gather_fusion
  551.9 1.2 gather_fusion.1
  553.2 4.9 select_reduce_fusion.2
  558.3 3.1 gather_fusion
  561.4 1.2 gather_fusion.1
  562.7 4.9 select_reduce_fusion.2
  567.8 3.1 gather_fusion
  570.9 1.2 gather_fusion.1
  572.2 4.9 select_reduce_fusion.2
  577.3 3.1 gather_fusion
  580.4 1.2 gather_fusion.1
  581.7 4.9 select_reduce_fusion.2
  586.8 3.1 gather_fusion
  589.8 1.2 gather_fusion.1
  591.2 4.9 select_reduce_fusion.2
  596.3 3.1 gather_fusion
  599.3 1.2 gather_fusion.1
  600.7 4.9 select_reduce_fusion.2
  605.8 3.1 gather_fusion
  608.8 1.2 gather_fusion.1
  610.1 4.9 select_reduce_fusion.2
  615.2 3.1 gather_fusion
  618.3 1.2 gather_fusion.1
  619.6 4.9 select_reduce_fusion.2
  624.9 1.1 copy.65
  626.0 5.5 all-to-all-start.4
  631.6 14.0 %all-to-all-done.4 = f32[64,8,2]{1,2,0:T(2,128)S(1)} async-done(((f32[64,8,2]{1,2,0:T(2,128)}), f32[64,8,2]{1,2,0:T(2,128)S(1)}, u32[]{:S(2)}, u32[]{:S(2)}) %all-to-all-start.4) | async-done | bytes 4128 | tf_op jit(solution)/shard_map/all_to_all | solution.py:90
  645.6 0.6 constant_dynamic-slice_fusion.1
  646.2 0.5 copy.66
  646.7 4.2 collective-permute-start
  650.9 2.2 collective-permute-start.1
  653.1 3.3 collective-permute-start.2
  656.4 2.4 collective-permute-start.3
  658.8 4.8 collective-permute-start.4
  663.8 2.8 collective-permute-start.5
  666.6 0.5 copy.67
  667.3 3.8 collective-permute-start.6
  671.1 0.5 copy.68
  671.8 0.5 copy.69
  672.4 0.5 copy.70
  673.1 0.5 copy.71
  673.7 0.5 copy.72
  674.4 0.5 copy.73
  675.2 2.3 gather_fusion.4
  677.5 0.7 copy.74
  (88 shorter events, 4.6 us)
Async XLA Ops:
  0.0 31.2 %copy-start = (bf16[32,32,128]{2,1,0:T(8,128)(2,1)S(1)}, bf16[32,32,128]{2,1,0:T(8,128)(2,1)}, u32[]{:S(2)}) copy-start(bf16[32,32,128]{2,1,0:T(8,128)(2,1)} %param.6) | copy-start | bytes 786436
  11.9 33.3 %all-to-all-start = ((s32[64,8,2]{1,2,0:T(2,128)}), s32[64,8,2]{1,2,0:T(2,128)S(1)}, u32[]{:S(2)}, u32[]{:S(2)}) async-start(s32[64,8,2]{1,2,0:T(2,128)} %copy.60), calls=%async_computation | async-start | bytes 131072 | tf_op jit(solution)/shard_map/all_to_all | solution.py:78
  45.2 371.7 %all-to-all-start.2 = ((bf16[64,8,2,32,128]{4,3,2,1,0:T(8,128)(2,1)}), bf16[64,8,2,32,128]{4,3,2,1,0:T(8,128)(2,1)}, u32[]{:S(2)}, u32[]{:S(2)}) async-start(bf16[64,8,2,32,128]{4,3,2,1,0:T(8,128)(2,1)} %bitcast.22), calls=%async_computation.2 | async-start | bytes 16777216 | tf_op jit(solution)/shard_map/all_to_all | solution.py:71
  416.9 23.5 %all-to-all-start.1 = ((s32[8,1,128]{2,1,0:T(1,128)}), s32[8,1,128]{2,1,0:T(1,128)S(1)}, u32[]{:S(2)}, u32[]{:S(2)}) async-start(s32[8,1,128]{2,1,0:T(1,128)} %reshape.245), calls=%async_computation.1 | async-start | bytes 8192 | tf_op jit(solution)/shard_map/all_to_all | solution.py:77
  440.4 98.8 %all-to-all-start.3 = ((bf16[64,8,2,32,128]{4,3,2,0,1:T(8,128)(2,1)}), bf16[64,8,2,32,128]{4,3,2,0,1:T(8,128)(2,1)}, u32[]{:S(2)}, u32[]{:S(2)}) async-start(bf16[64,8,2,32,128]{4,3,2,0,1:T(8,128)(2,1)} %copy.63), calls=%async_computation.3 | async-start | bytes 16777216 | tf_op jit(solution)/shard_map/all_to_all | solution.py:70
  447.1 101.8 %copy-start.1 = (s32[64]{0:T(128)S(1)}, s32[64]{0:T(128)}, u32[]{:S(2)}) copy-start(s32[64]{0:T(128)} %param.8) | copy-start | bytes 772
  447.1 101.8 %copy-start.2 = (bf16[64,128,128]{2,1,0:T(8,128)(2,1)S(1)}, bf16[64,128,128]{2,1,0:T(8,128)(2,1)}, u32[]{:S(2)}) copy-start(bf16[64,128,128]{2,1,0:T(8,128)(2,1)} %param.7) | copy-start | bytes 6291460
  626.0 19.6 %all-to-all-start.4 = ((f32[64,8,2]{1,2,0:T(2,128)}), f32[64,8,2]{1,2,0:T(2,128)S(1)}, u32[]{:S(2)}, u32[]{:S(2)}) async-start(f32[64,8,2]{1,2,0:T(2,128)} %copy.65), calls=%async_computation.4 | async-start | bytes 131072 | tf_op jit(solution)/shard_map/all_to_all | solution.py:90
  646.7 17.1 %collective-permute-start = (f32[64,1,2]{1,2,0:T(2,128)S(1)}, f32[64,1,2]{1,2,0:T(2,128)S(1)}, u32[]{:S(2)}, u32[]{:S(2)}) collective-permute-start(f32[64,1,2]{1,2,0:T(2,128)S(1)} %get-tuple-element.56), channel_id=1, source_target_pairs={{0,1},{1,0},{2,3},{3,2},{4,5},{5,4},{6,7},{7,6},{8,9},{9,8},{10,11... | collective-permute-start | bytes 1544 | tf_op jit(solution)/shard_map/ppermute | solution.py:19
  650.9 16.3 %collective-permute-start.1 = (f32[64,1,2]{1,2,0:T(2,128)S(1)}, f32[64,1,2]{1,2,0:T(2,128)S(1)}, u32[]{:S(2)}, u32[]{:S(2)}) collective-permute-start(f32[64,1,2]{1,2,0:T(2,128)S(1)} %get-tuple-element.55), channel_id=1, source_target_pairs={{0,2},{1,3},{2,0},{3,1},{4,6},{5,7},{6,4},{7,5},{8,10},{9,11},{10,... | collective-permute-start | bytes 1544 | tf_op jit(solution)/shard_map/ppermute | solution.py:19
  653.1 18.6 %collective-permute-start.2 = (f32[64,1,2]{1,2,0:T(2,128)S(1)}, f32[64,1,2]{1,2,0:T(2,128)S(1)}, u32[]{:S(2)}, u32[]{:S(2)}) collective-permute-start(f32[64,1,2]{1,2,0:T(2,128)S(1)} %get-tuple-element.54), channel_id=1, source_target_pairs={{0,3},{1,2},{2,1},{3,0},{4,7},{5,6},{6,5},{7,4},{8,11},{9,10},{10,... | collective-permute-start | bytes 1544 | tf_op jit(solution)/shard_map/ppermute | solution.py:19
  656.4 16.0 %collective-permute-start.3 = (f32[64,1,2]{1,2,0:T(2,128)S(1)}, f32[64,1,2]{1,2,0:T(2,128)S(1)}, u32[]{:S(2)}, u32[]{:S(2)}) collective-permute-start(f32[64,1,2]{1,2,0:T(2,128)S(1)} %get-tuple-element.53), channel_id=1, source_target_pairs={{0,4},{1,5},{2,6},{3,7},{4,0},{5,1},{6,2},{7,3},{8,12},{9,13},{10,... | collective-permute-start | bytes 1544 | tf_op jit(solution)/shard_map/ppermute | solution.py:19
  658.8 14.3 %collective-permute-start.4 = (f32[64,1,2]{1,2,0:T(2,128)S(1)}, f32[64,1,2]{1,2,0:T(2,128)S(1)}, u32[]{:S(2)}, u32[]{:S(2)}) collective-permute-start(f32[64,1,2]{1,2,0:T(2,128)S(1)} %get-tuple-element.52), channel_id=1, source_target_pairs={{0,5},{1,4},{2,7},{3,6},{4,1},{5,0},{6,3},{7,2},{8,13},{9,12},{10,... | collective-permute-start | bytes 1544 | tf_op jit(solution)/shard_map/ppermute | solution.py:19
  663.8 9.9 %collective-permute-start.5 = (f32[64,1,2]{1,2,0:T(2,128)S(1)}, f32[64,1,2]{1,2,0:T(2,128)S(1)}, u32[]{:S(2)}, u32[]{:S(2)}) collective-permute-start(f32[64,1,2]{1,2,0:T(2,128)S(1)} %get-tuple-element.51), channel_id=1, source_target_pairs={{0,6},{1,7},{2,4},{3,5},{4,2},{5,3},{6,0},{7,1},{8,14},{9,15},{10,... | collective-permute-start | bytes 1544 | tf_op jit(solution)/shard_map/ppermute | solution.py:19
  667.3 7.1 %collective-permute-start.6 = (f32[64,1,2]{1,2,0:T(2,128)S(1)}, f32[64,1,2]{1,2,0:T(2,128)S(1)}, u32[]{:S(2)}, u32[]{:S(2)}) collective-permute-start(f32[64,1,2]{1,2,0:T(2,128)S(1)} %get-tuple-element.50), channel_id=1, source_target_pairs={{0,7},{1,6},{2,5},{3,4},{4,3},{5,2},{6,1},{7,0},{8,15},{9,14},{10,... | collective-permute-start | bytes 1544 | tf_op jit(solution)/shard_map/ppermute | solution.py:19
